TPU v7x, 32 devices: a whole 2x2x4 slice. The times are simulated.
32 devices in a mesh: groups: 2 (over x), vel: 16 (over z, y, core).
Axes of the slice: x: 2, y: 2, z: 4, core: 2. Of those that a mesh axis runs over, the one named last changes fastest.
Arguments:
- signal: bfloat16 [32, 8, 512], P(('groups', 'vel')), parts along dimension 0, may hold values from -6 to 6
- weight: bfloat16 [32, 8, 512], P(('groups', 'vel')), parts along dimension 0, may hold values from 0.25 to 4
- shifts: int32 [16, 16, 2], P('vel'), may hold values from -15 to 15, as said below
- phases: int32 [16, 16, 2], P('vel'), may hold values from 0 to 7, as said below
Outputs:
- likelihood: float32 [32, 8, 512], P(('groups', 'vel')), parts along dimension 0
- best_likelihood: float32 [16, 512], P('groups'), parts along dimension 0
There are 2 independent parts, one for each index of `groups`. A program takes and returns all parts, laid end to end along the dimension named above; an argument that names none is the same for every part. Nothing has to cross between parts.
Inputs may be any that keep to these rules, and one draw needn't show every extreme that they name: shifts[v, e] = floor(o / 8) of offsets o in eighths of a pixel that grow with the exposure index e for each velocity: column offset a_v e with a_v in -8..8, row offset floor(b_v e / 16) with b_v in -8..8; some velocity has a_v = 8 and another a_v = -8. phases[v, e] = the same offsets modulo 8.
All inputs are finite; a program needn't handle non-finite values.
Results may differ from a plain program's by a relative error of at most 0.0003.
Values may be sent and summed in bfloat16 or wider, within the bound.
A program may use at most 64 MiB of HBM per device.

v0:
```python
import jax
import jax.numpy as jnp
from jax import lax
from jax.sharding import PartitionSpec as P


def tap_table():
    fraction = jnp.arange(8, dtype=jnp.float32) / 8.0
    position = (jnp.arange(6, dtype=jnp.int32) - 2).astype(jnp.float32)
    distance = position[None, :] - fraction[:, None]
    raw_taps = jnp.sinc(distance) * jnp.sinc(distance / 3.0)
    return (raw_taps / jnp.sum(raw_taps, axis=1, keepdims=True)).astype(jnp.float32)


def pick_taps(coefficients, phase_index):
    choose = (jnp.arange(coefficients.shape[0], dtype=jnp.int32) == phase_index).astype(jnp.float32)
    return jnp.sum(choose[:, None] * coefficients, axis=0)


def place_pair(padded, shift_pair, phase_pair, coefficients, margin, columns, reach):
    height = padded.shape[1]
    col_taps = pick_taps(coefficients, phase_pair[1])
    row_taps = pick_taps(coefficients, phase_pair[0])
    anchor = shift_pair[0] * 0
    col_start = reach + shift_pair[1] - 2
    slab = lax.dynamic_slice(padded, (anchor, anchor, col_start), (2, height, columns + 5)).astype(
        jnp.float32
    )
    row_pass = sum(
        (
            col_taps[tap_index] * slab[:, :, tap_index : tap_index + columns]
            for tap_index in range(6)
        )
    )
    tall = jnp.pad(row_pass, ((0, 0), (margin, margin), (0, 0)))
    row_start = margin + shift_pair[0] - 2
    slab_rows = lax.dynamic_slice(tall, (anchor, row_start, anchor), (2, height + 5, columns))
    return sum(
        (
            row_taps[tap_index] * slab_rows[:, tap_index : tap_index + height, :]
            for tap_index in range(6)
        )
    )


def place_block(padded, shift_block, phase_block, coefficients, margin, columns, reach):
    placed = jax.vmap(
        lambda image, shift_pair, phase_pair: place_pair(
            image, shift_pair, phase_pair, coefficients, margin, columns, reach
        )
    )(padded, shift_block, phase_block)
    return jnp.sum(placed, axis=0)


def stack_velocities(padded, shift_rows, phase_rows, coefficients, margin, columns, reach):
    count = padded.shape[0]
    height = padded.shape[2]
    block = 32 if count % 32 == 0 else count
    groups_count = count // block

    def one_velocity(inputs):
        shift_set, phase_set = inputs
        if groups_count == 1:
            return place_block(padded, shift_set, phase_set, coefficients, margin, columns, reach)
        blocked = padded.reshape((groups_count, block) + padded.shape[1:])
        shift_blocks = shift_set.reshape((groups_count, block, 2))
        phase_blocks = phase_set.reshape((groups_count, block, 2))

        def add_block(total, item):
            images, shift_block, phase_block = item
            return (
                total
                + place_block(
                    images, shift_block, phase_block, coefficients, margin, columns, reach
                ),
                None,
            )

        start = jnp.zeros((2, height, columns), jnp.float32)
        total, unused = lax.scan(add_block, start, (blocked, shift_blocks, phase_blocks))
        return total

    return lax.map(one_velocity, (shift_rows, phase_rows))


def widen(signal_part, weight_part, reach):
    images = jnp.stack([signal_part, weight_part], axis=1)
    return jnp.pad(images, ((0, 0), (0, 0), (0, 0), (reach, reach)))


def body(signal, weight, shifts, phases):
    coefficients = tap_table()
    columns = signal.shape[2]
    margin = shifts.shape[1] // 16 + 6
    reach = shifts.shape[1] + 3
    gathered_signal, gathered_weight = (
        lax.all_gather(signal, "vel", axis=0, tiled=True),
        lax.all_gather(weight, "vel", axis=0, tiled=True),
    )
    summed = stack_velocities(
        widen(gathered_signal, gathered_weight, reach),
        shifts,
        phases,
        coefficients,
        margin,
        columns,
        reach,
    )
    likelihood = summed[:, 0] / jnp.sqrt(jnp.maximum(summed[:, 1], 1.0))
    best_likelihood = lax.pmax(jnp.max(likelihood, axis=0), "vel")
    return (likelihood, best_likelihood)


def solution(mesh):
    in_specs = (
        P(("groups", "vel"), None, None),
        P(("groups", "vel"), None, None),
        P("vel", None, None),
        P("vel", None, None),
    )
    out_specs = (P(("groups", "vel"), None, None), P("groups", None))
    return jax.shard_map(body, mesh=mesh, in_specs=in_specs, out_specs=out_specs, check_vma=False)
```

profile of v0, /device:TPU:0, one launch (start us, length us, event | category | flops | bytes accessed | tf_op | source)
XLA Modules:
  0.0 174.9 jit_solution(8193985154500921316)
XLA Ops:
  0.6 23.7 %all_gather.7 = bf16[16,8,512]{2,1,0:T(8,128)(2,1)S(1)} all-gather(bf16[1,8,512]{2,1,0:T(8,128)(2,1)} %param.6), channel_id=1, replica_groups=mesh['groups'=2,'vel'=16] {'vel'}, dimensions={0}, use_global_device_ids=true | all-gather | bytes 139264 | tf_op jit(solution)/shard_map/all_gather | solution.py:98
  24.3 7.5 %copy.24 = bf16[16,1,8,512]{2,1,0,3:T(2,128)(2,1)} copy(bf16[16,1,8,512]{3,2,0,1:T(8,128)(2,1)S(1)} %bitcast.42) | data formatting | bytes 262144 | tf_op jit(solution)/shard_map/stack | solution.py:87
  31.9 18.0 %all_gather.6 = bf16[16,8,512]{2,1,0:T(8,128)(2,1)S(1)} all-gather(bf16[1,8,512]{2,1,0:T(8,128)(2,1)} %param.5), channel_id=1, replica_groups=mesh['groups'=2,'vel'=16] {'vel'}, dimensions={0}, use_global_device_ids=true | all-gather | bytes 139264 | tf_op jit(solution)/shard_map/all_gather | solution.py:97
  49.9 7.5 %copy.23 = bf16[16,1,8,512]{2,1,0,3:T(2,128)(2,1)} copy(bf16[16,1,8,512]{3,2,0,1:T(8,128)(2,1)S(1)} %bitcast.43) | data formatting | bytes 262144 | tf_op jit(solution)/shard_map/stack | solution.py:87
  57.4 0.0 copy-start
  57.4 28.2 %select_maximum_fusion = bf16[16,2,8,550]{2,1,0,3:T(2,128)(2,1)} fusion(bf16[16,1,8,512]{2,1,0,3:T(2,128)(2,1)} %copy.24, bf16[16,1,8,512]{2,1,0,3:T(2,128)(2,1)} %copy.23), kind=kLoop, calls=%fused_computation.3 | loop fusion | flops 1267200 | bytes 543744 | tf_op jit(solution)/shard_map/stack | solution.py:87
  85.6 0.0 copy-start.1
  85.6 0.0 copy-done
  85.6 15.2 %gather_fusion = bf16[16,2,8,517]{2,1,3,0:T(2,128)(2,1)} fusion(bf16[16,2,8,550]{2,1,0,3:T(2,128)(2,1)} %select_maximum_fusion, s32[16]{0:T(128)S(1)} %get-tuple-element.42), kind=kCustom, calls=%fused_computation | custom fusion | bytes 529664 | tf_op jit(solution)/shard_map/while/body/eval_jaxpr/vmap()/gather | solution.py:26
  100.8 9.2 %copy.25 = bf16[16,2,8,517]{3,2,1,0:T(8,128)(2,1)S(1)} copy(bf16[16,2,8,517]{2,1,3,0:T(2,128)(2,1)} %gather_fusion) | data formatting | bytes 529408 | tf_op jit(solution)/shard_map/while/body/eval_jaxpr/vmap()/gather | solution.py:26
  110.0 0.1 convert_element_type.40
  110.1 0.2 fusion.58
  110.3 0.1 broadcast_divide_fusion
  110.4 0.1 copy.22
  110.5 0.0 copy-done.1
  110.5 0.1 multiply_reduce_fusion.1
  110.6 0.9 fusion.5
  111.5 0.4 copy.29
  111.9 0.5 pad.11.clone
  112.4 1.5 gather_fusion.1
  113.9 1.2 fusion.10
  115.2 0.6 copy.27
  115.8 59.1 %pmax.7 = f32[8,512]{1,0:T(8,128)} all-reduce(f32[8,512]{1,0:T(8,128)S(1)} %bitcast.46), channel_id=1, replica_groups=mesh['groups'=2,'vel'=16] {'vel'}, use_global_device_ids=true, to_apply=%region_4.6 | all-reduce | flops 4096 | bytes 32768 | tf_op jit(solution)/shard_map/pmax | solution.py:110
  (10 shorter events, 0.1 us)
Async XLA Ops:
  57.4 28.2 %copy-start = (s32[1,16,2]{1,2,0:T(2,128)S(1)}, s32[1,16,2]{1,2,0:T(2,128)}, u32[]{:S(2)}) copy-start(s32[1,16,2]{1,2,0:T(2,128)} %param.7) | copy-start | bytes 388
  85.6 24.9 %copy-start.1 = (s32[1,16,2]{1,2,0:T(2,128)S(1)}, s32[1,16,2]{1,2,0:T(2,128)}, u32[]{:S(2)}) copy-start(s32[1,16,2]{1,2,0:T(2,128)} %param.8) | copy-start | bytes 388
where the time goes:
time: 175 us
  blocking collectives  101 us (58%)
  local copies, waits for them, and re-layouts  42.5 us (24%)
  other arithmetic  30.8 us (18%)
    pmax x1, blocking collectives, body(): best_likelihood = lax.pmax(jnp.max(likelihood, axis=0), 'vel')  59.1 us
    another operation x1, other arithmetic, widen(): images = jnp.stack([signal_part, weight_part], axis=1)  28.2 us
    gather x2, local copies, waits for them, and re-layouts, place_pair(): lax.dynamic_slice(padded, (anchor, anchor, col_start), (2, height, column...  24.4 us
    all_gather x1, blocking collectives, body(): lax.all_gather(weight, 'vel', axis=0, tiled=True)  23.7 us
    all_gather x1, blocking collectives, body(): lax.all_gather(signal, 'vel', axis=0, tiled=True)  18 us
    another operation x2, local copies, waits for them, and re-layouts, widen(): images = jnp.stack([signal_part, weight_part], axis=1)  15 us

commit v1 on v0

--- a/solution.py
+++ b/solution.py
@@ -1,7 +1,37 @@
+import functools
 import jax
 import jax.numpy as jnp
 from jax import lax
 from jax.sharding import PartitionSpec as P
+
+
+def expand_trails(field, axis_no):
+    field = jnp.moveaxis(field, 0, axis_no)
+    field_out = field.shape
+    built = field.reshape(
+        *field_out[:axis_no], field_out[axis_no] * field_out[axis_no + 1], *field_out[axis_no + 2 :]
+    )
+    return built
+
+
+def touch_indices(my_tile, shard_axis, at_axis):
+    width = jax.lax.axis_size(shard_axis)
+    series = tuple(((k0, (k0 + 1) % width) for k0 in range(width)))
+    block_list = tuple(((b, k) for k, b in series))
+    z_new, g_now = ([], [])
+    for u in range(width - 1):
+        if u % 2 == 0:
+            z_new.append(jax.lax.ppermute(z_new[-1] if z_new else my_tile, shard_axis, series))
+        else:
+            g_now.append(jax.lax.ppermute(g_now[-1] if g_now else my_tile, shard_axis, block_list))
+    now = jnp.stack([*z_new[::-1], my_tile, *g_now], axis=0)
+    odd = jax.lax.axis_index(shard_axis) - len(z_new)
+    now = now[(jnp.arange(width) - odd) % width]
+    then = expand_trails(now, at_axis)
+    return then
+
+
+prepare_digits_on = functools.partial(touch_indices, shard_axis="vel", at_axis=0)
 
 
 def tap_table():
@@ -94,7 +124,7 @@
     margin = shifts.shape[1] // 16 + 6
     reach = shifts.shape[1] + 3
     gathered_signal, gathered_weight = (
-        lax.all_gather(signal, "vel", axis=0, tiled=True),
+        prepare_digits_on(signal),
         lax.all_gather(weight, "vel", axis=0, tiled=True),
     )
     summed = stack_velocities(

time: 175 us -> 199 us (1.14)
  starting transfers between devices: 0 us -> 28.9 us
  blocking collectives: 101 us -> 80.5 us
  waiting for transfers between devices: 0 us -> 13.1 us
    ppermute x0 -> x15, starting transfers between devices: none -> 28.9 us  [the longest x7 28.4 us: touch_indices(): jax.lax.ppermute(g_now[-1] if g_now else my_tile, shard_axis, block_list)]
    all_gather x1 -> x0, blocking collectives: 18 us -> none  [body(): lax.all_gather(signal, 'vel', axis=0, tiled=True)]
    ppermute x0 -> x15, waiting for transfers between devices: none -> 13.1 us  [the longest x8 10.1 us: touch_indices(): jax.lax.ppermute(z_new[-1] if z_new else my_tile, shard_axis, series)]
    gather x0 -> x2, local copies, waits for them, and re-layouts: none -> 8.1 us  [touch_indices(): now = now[(jnp.arange(width) - odd) % width]]
    another operation x2 -> x1, local copies, waits for them, and re-layouts: 15 us -> 7.56 us  [widen(): images = jnp.stack([signal_part, weight_part], axis=1)]
    all_gather x1, blocking collectives: 23.7 us -> 18.6 us  [body(): lax.all_gather(weight, 'vel', axis=0, tiled=True)]
    pmax x1, blocking collectives: 59.1 us -> 61.9 us  [body(): best_likelihood = lax.pmax(jnp.max(likelihood, axis=0), 'vel')]
  transfers between devices with their start and end apart: 0 -> 15, of which waited for: 0 -> 11; matrix products, arithmetic and copies ran while one was open for 0% -> 5% of each run, Pallas kernels for 0% -> 0%
where the time goes in v1:
time: 199 us
  blocking collectives  80.5 us (40%)
  local copies, waits for them, and re-layouts  44 us (22%)
  other arithmetic  31.6 us (16%)
  starting transfers between devices  28.9 us (15%)
  waiting for transfers between devices  13.1 us (7%)
    pmax x1, blocking collectives, body(): best_likelihood = lax.pmax(jnp.max(likelihood, axis=0), 'vel')  61.9 us
    ppermute x7, starting transfers between devices, touch_indices(): jax.lax.ppermute(g_now[-1] if g_now else my_tile, shard_axis, block_list)  28.4 us
    another operation x1, other arithmetic, widen(): images = jnp.stack([signal_part, weight_part], axis=1)  28.2 us
    gather x2, local copies, waits for them, and re-layouts, place_pair(): lax.dynamic_slice(padded, (anchor, anchor, col_start), (2, height, column...  24.4 us
    all_gather x1, blocking collectives, body(): lax.all_gather(weight, 'vel', axis=0, tiled=True)  18.6 us
    ppermute x8, waiting for transfers between devices, touch_indices(): jax.lax.ppermute(z_new[-1] if z_new else my_tile, shard_axis, series)  10.1 us
    gather x2, local copies, waits for them, and re-layouts, touch_indices(): now = now[(jnp.arange(width) - odd) % width]  8.1 us
    another operation x1, local copies, waits for them, and re-layouts, widen(): images = jnp.stack([signal_part, weight_part], axis=1)  7.56 us
  transfers between devices with their start and end apart: 15, of which 11 were waited for; matrix products, arithmetic and copies ran while one was open for 5% of the time, Pallas kernels for 0%

profile of v1, /device:TPU:0, one launch (start us, length us, event | category | flops | bytes accessed | tf_op | source)
XLA Modules:
  0.0 199.0 jit_solution(17865814947957237593)
XLA Ops:
  0.6 0.5 collective-permute-start
  1.2 5.0 %collective-permute-start.8 = (bf16[1,8,512]{2,1,0:T(8,128)(2,1)}, bf16[1,8,512]{2,1,0:T(8,128)(2,1)S(1)}, u32[]{:S(2)}, u32[]{:S(2)}) collective-permute-start(bf16[1,8,512]{2,1,0:T(8,128)(2,1)} %param.5), channel_id=1, source_target_pairs={{1,0},{2,1},{3,2},{4,3},{5,4},{6,5},{7,6},{8,7},{9,8},{10,9},{11,1... | collective-permute-start | bytes 24584 | tf_op jit(solution)/shard_map/ppermute | solution.py:26
  6.2 0.8 slice_bitcast_fusion.11
  7.0 0.2 fusion.58
  7.2 0.1 broadcast_divide_fusion
  7.3 0.1 copy.60
  7.4 0.3 collective-permute-done
  7.7 0.0 collective-permute-start.1
  7.7 0.1 multiply_reduce_fusion.1
  7.8 5.8 %collective-permute-done.1 = bf16[1,8,512]{2,1,0:T(8,128)(2,1)S(1)} collective-permute-done((bf16[1,8,512]{2,1,0:T(8,128)(2,1)S(1)}, bf16[1,8,512]{2,1,0:T(8,128)(2,1)S(1)}, u32[]{:S(2)}, u32[]{:S(2)}) %collective-permute-start.1) | collective-permute-done | bytes 8224 | tf_op jit(solution)/shard_map/ppermute | solution.py:24
  13.6 0.0 collective-permute-start.2
  13.6 0.0 collective-permute-done.8
  13.6 4.5 %collective-permute-start.9 = (bf16[1,8,512]{2,1,0:T(8,128)(2,1)S(1)}, bf16[1,8,512]{2,1,0:T(8,128)(2,1)S(1)}, u32[]{:S(2)}, u32[]{:S(2)}) collective-permute-start(bf16[1,8,512]{2,1,0:T(8,128)(2,1)S(1)} %collective-permute-done.8), channel_id=1, source_target_pairs={{1,0},{2,1},{3,2},{4,3},{5,4},{6,5},{7,6},{8,7},{9,8},{10,9},{11,1... | collective-permute-start | bytes 24584 | tf_op jit(solution)/shard_map/ppermute | solution.py:26
  18.1 1.3 collective-permute-done.2
  19.3 0.0 collective-permute-start.3
  19.4 0.1 collective-permute-done.9
  19.4 4.4 %collective-permute-start.10 = (bf16[1,8,512]{2,1,0:T(8,128)(2,1)S(1)}, bf16[1,8,512]{2,1,0:T(8,128)(2,1)S(1)}, u32[]{:S(2)}, u32[]{:S(2)}) collective-permute-start(bf16[1,8,512]{2,1,0:T(8,128)(2,1)S(1)} %collective-permute-done.9), channel_id=1, source_target_pairs={{1,0},{2,1},{3,2},{4,3},{5,4},{6,5},{7,6},{8,7},{9,8},{10,9},{11,1... | collective-permute-start | bytes 24584 | tf_op jit(solution)/shard_map/ppermute | solution.py:26
  23.9 1.3 collective-permute-done.3
  25.1 0.0 collective-permute-start.4
  25.1 0.8 or_bitcast_fusion
  25.9 4.5 %collective-permute-start.11 = (bf16[1,8,512]{2,1,0:T(8,128)(2,1)S(1)}, bf16[1,8,512]{2,1,0:T(8,128)(2,1)S(1)}, u32[]{:S(2)}, u32[]{:S(2)}) collective-permute-start(bf16[1,8,512]{2,1,0:T(8,128)(2,1)S(1)} %collective-permute-done.10), channel_id=1, source_target_pairs={{1,0},{2,1},{3,2},{4,3},{5,4},{6,5},{7,6},{8,7},{9,8},{10,9},{11,1... | collective-permute-start | bytes 24584 | tf_op jit(solution)/shard_map/ppermute | solution.py:26
  30.4 0.5 collective-permute-done.4
  30.9 0.9 collective-permute-done.11
  31.8 4.4 %collective-permute-start.12 = (bf16[1,8,512]{2,1,0:T(8,128)(2,1)S(1)}, bf16[1,8,512]{2,1,0:T(8,128)(2,1)S(1)}, u32[]{:S(2)}, u32[]{:S(2)}) collective-permute-start(bf16[1,8,512]{2,1,0:T(8,128)(2,1)S(1)} %collective-permute-done.11), channel_id=1, source_target_pairs={{1,0},{2,1},{3,2},{4,3},{5,4},{6,5},{7,6},{8,7},{9,8},{10,9},{11,1... | collective-permute-start | bytes 24584 | tf_op jit(solution)/shard_map/ppermute | solution.py:26
  36.2 0.5 collective-permute-done.5
  36.7 0.9 collective-permute-done.12
  37.5 4.4 %collective-permute-start.13 = (bf16[1,8,512]{2,1,0:T(8,128)(2,1)S(1)}, bf16[1,8,512]{2,1,0:T(8,128)(2,1)S(1)}, u32[]{:S(2)}, u32[]{:S(2)}) collective-permute-start(bf16[1,8,512]{2,1,0:T(8,128)(2,1)S(1)} %collective-permute-done.12), channel_id=1, source_target_pairs={{1,0},{2,1},{3,2},{4,3},{5,4},{6,5},{7,6},{8,7},{9,8},{10,9},{11,1... | collective-permute-start | bytes 24584 | tf_op jit(solution)/shard_map/ppermute | solution.py:26
  41.9 0.5 collective-permute-done.6
  42.4 0.0 collective-permute-start.7
  42.4 18.6 %all_gather.3 = bf16[16,8,512]{2,1,0:T(8,128)(2,1)S(1)} all-gather(bf16[1,8,512]{2,1,0:T(8,128)(2,1)} %param.6), channel_id=1, replica_groups=mesh['groups'=2,'vel'=16] {'vel'}, dimensions={0}, use_global_device_ids=true | all-gather | bytes 139264 | tf_op jit(solution)/shard_map/all_gather | solution.py:128
  61.0 7.6 %copy.75 = bf16[16,1,8,512]{2,1,0,3:T(2,128)(2,1)} copy(bf16[16,1,8,512]{3,2,0,1:T(8,128)(2,1)S(1)} %bitcast.104) | data formatting | bytes 262144 | tf_op jit(solution)/shard_map/stack | solution.py:117
  68.6 0.0 collective-permute-done.13
  68.6 1.1 collective-permute-start.14
  69.7 0.0 collective-permute-done.7
  69.9 1.2 collective-permute-done.14
  71.1 0.6 gather_fusion
  71.7 7.5 %copy.74 = bf16[16,1,8,512]{2,1,0,3:T(2,128)(2,1)} copy(bf16[16,1,8,512]{3,2,0,1:T(8,128)(2,1)S(1)} %bitcast.103) | data formatting | bytes 262144 | tf_op jit(solution)/shard_map/gather | solution.py:29
  79.2 28.2 %select_maximum_fusion = bf16[16,2,8,550]{2,1,0,3:T(2,128)(2,1)} fusion(bf16[16,1,8,512]{2,1,0,3:T(2,128)(2,1)} %copy.75, bf16[16,1,8,512]{2,1,0,3:T(2,128)(2,1)} %copy.74), kind=kLoop, calls=%fused_computation.4 | loop fusion | flops 1267200 | bytes 543744 | tf_op jit(solution)/shard_map/stack | solution.py:117
  107.4 15.2 %gather_fusion.1 = bf16[16,2,8,517]{2,1,3,0:T(2,128)(2,1)} fusion(bf16[16,2,8,550]{2,1,0,3:T(2,128)(2,1)} %select_maximum_fusion, s32[16]{0:T(128)S(1)} %get-tuple-element.42), kind=kCustom, calls=%fused_computation.1 | custom fusion | bytes 529664 | tf_op jit(solution)/shard_map/while/body/eval_jaxpr/vmap()/gather | solution.py:56
  122.6 9.2 %copy.76 = bf16[16,2,8,517]{3,2,1,0:T(8,128)(2,1)S(1)} copy(bf16[16,2,8,517]{2,1,3,0:T(2,128)(2,1)} %gather_fusion.1) | data formatting | bytes 529408 | tf_op jit(solution)/shard_map/while/body/eval_jaxpr/vmap()/gather | solution.py:56
  131.8 0.1 convert_element_type.40
  131.9 0.9 fusion.5
  132.8 0.4 copy.80
  133.2 0.5 pad.11.clone
  133.7 1.5 gather_fusion.2
  135.2 1.2 fusion.10
  136.5 61.9 %pmax.7 = f32[8,512]{1,0:T(8,128)} all-reduce(f32[8,512]{1,0:T(8,128)S(1)} %bitcast.108), channel_id=1, replica_groups=mesh['groups'=2,'vel'=16] {'vel'}, use_global_device_ids=true, to_apply=%region_4.6 | all-reduce | flops 4096 | bytes 32768 | tf_op jit(solution)/shard_map/pmax | solution.py:140
  198.4 0.6 copy.78
  (31 shorter events, 0.2 us)
Async XLA Ops:
  0.6 69.2 %copy-start = (bf16[1,8,512]{2,1,0:T(8,128)(2,1)S(1)}, bf16[1,8,512]{2,1,0:T(8,128)(2,1)}, u32[]{:S(2)}) copy-start(bf16[1,8,512]{2,1,0:T(8,128)(2,1)} %param.5) | copy-start | bytes 24580
  0.6 7.1 %collective-permute-start = (bf16[1,8,512]{2,1,0:T(8,128)(2,1)}, bf16[1,8,512]{2,1,0:T(8,128)(2,1)S(1)}, u32[]{:S(2)}, u32[]{:S(2)}) collective-permute-start(bf16[1,8,512]{2,1,0:T(8,128)(2,1)} %param.5), channel_id=1, source_target_pairs={{0,1},{1,2},{2,3},{3,4},{4,5},{5,6},{6,7},{7,8},{8,9},{9,10},{10,1... | collective-permute-start | bytes 24584 | tf_op jit(solution)/shard_map/ppermute | solution.py:24
  1.2 12.4 %collective-permute-start.8 = (bf16[1,8,512]{2,1,0:T(8,128)(2,1)}, bf16[1,8,512]{2,1,0:T(8,128)(2,1)S(1)}, u32[]{:S(2)}, u32[]{:S(2)}) collective-permute-start(bf16[1,8,512]{2,1,0:T(8,128)(2,1)} %param.5), channel_id=1, source_target_pairs={{1,0},{2,1},{3,2},{4,3},{5,4},{6,5},{7,6},{8,7},{9,8},{10,9},{11,1... | collective-permute-start | bytes 24584 | tf_op jit(solution)/shard_map/ppermute | solution.py:26
  7.7 5.9 %collective-permute-start.1 = (bf16[1,8,512]{2,1,0:T(8,128)(2,1)S(1)}, bf16[1,8,512]{2,1,0:T(8,128)(2,1)S(1)}, u32[]{:S(2)}, u32[]{:S(2)}) collective-permute-start(bf16[1,8,512]{2,1,0:T(8,128)(2,1)S(1)} %collective-permute-done), channel_id=1, source_target_pairs={{0,1},{1,2},{2,3},{3,4},{4,5},{5,6},{6,7},{7,8},{8,9},{9,10},{10,1... | collective-permute-start | bytes 24584 | tf_op jit(solution)/shard_map/ppermute | solution.py:24
  13.6 5.8 %collective-permute-start.2 = (bf16[1,8,512]{2,1,0:T(8,128)(2,1)S(1)}, bf16[1,8,512]{2,1,0:T(8,128)(2,1)S(1)}, u32[]{:S(2)}, u32[]{:S(2)}) collective-permute-start(bf16[1,8,512]{2,1,0:T(8,128)(2,1)S(1)} %collective-permute-done.1), channel_id=1, source_target_pairs={{0,1},{1,2},{2,3},{3,4},{4,5},{5,6},{6,7},{7,8},{8,9},{9,10},{10,1... | collective-permute-start | bytes 24584 | tf_op jit(solution)/shard_map/ppermute | solution.py:24
  13.6 5.9 %collective-permute-start.9 = (bf16[1,8,512]{2,1,0:T(8,128)(2,1)S(1)}, bf16[1,8,512]{2,1,0:T(8,128)(2,1)S(1)}, u32[]{:S(2)}, u32[]{:S(2)}) collective-permute-start(bf16[1,8,512]{2,1,0:T(8,128)(2,1)S(1)} %collective-permute-done.8), channel_id=1, source_target_pairs={{1,0},{2,1},{3,2},{4,3},{5,4},{6,5},{7,6},{8,7},{9,8},{10,9},{11,1... | collective-permute-start | bytes 24584 | tf_op jit(solution)/shard_map/ppermute | solution.py:26
  19.3 5.8 %collective-permute-start.3 = (bf16[1,8,512]{2,1,0:T(8,128)(2,1)S(1)}, bf16[1,8,512]{2,1,0:T(8,128)(2,1)S(1)}, u32[]{:S(2)}, u32[]{:S(2)}) collective-permute-start(bf16[1,8,512]{2,1,0:T(8,128)(2,1)S(1)} %collective-permute-done.2), channel_id=1, source_target_pairs={{0,1},{1,2},{2,3},{3,4},{4,5},{5,6},{6,7},{7,8},{8,9},{9,10},{10,1... | collective-permute-start | bytes 24584 | tf_op jit(solution)/shard_map/ppermute | solution.py:24
  19.4 6.4 %collective-permute-start.10 = (bf16[1,8,512]{2,1,0:T(8,128)(2,1)S(1)}, bf16[1,8,512]{2,1,0:T(8,128)(2,1)S(1)}, u32[]{:S(2)}, u32[]{:S(2)}) collective-permute-start(bf16[1,8,512]{2,1,0:T(8,128)(2,1)S(1)} %collective-permute-done.9), channel_id=1, source_target_pairs={{1,0},{2,1},{3,2},{4,3},{5,4},{6,5},{7,6},{8,7},{9,8},{10,9},{11,1... | collective-permute-start | bytes 24584 | tf_op jit(solution)/shard_map/ppermute | solution.py:26
  25.1 5.8 %collective-permute-start.4 = (bf16[1,8,512]{2,1,0:T(8,128)(2,1)S(1)}, bf16[1,8,512]{2,1,0:T(8,128)(2,1)S(1)}, u32[]{:S(2)}, u32[]{:S(2)}) collective-permute-start(bf16[1,8,512]{2,1,0:T(8,128)(2,1)S(1)} %collective-permute-done.3), channel_id=1, source_target_pairs={{0,1},{1,2},{2,3},{3,4},{4,5},{5,6},{6,7},{7,8},{8,9},{9,10},{10,1... | collective-permute-start | bytes 24584 | tf_op jit(solution)/shard_map/ppermute | solution.py:24
  25.9 5.9 %collective-permute-start.11 = (bf16[1,8,512]{2,1,0:T(8,128)(2,1)S(1)}, bf16[1,8,512]{2,1,0:T(8,128)(2,1)S(1)}, u32[]{:S(2)}, u32[]{:S(2)}) collective-permute-start(bf16[1,8,512]{2,1,0:T(8,128)(2,1)S(1)} %collective-permute-done.10), channel_id=1, source_target_pairs={{1,0},{2,1},{3,2},{4,3},{5,4},{6,5},{7,6},{8,7},{9,8},{10,9},{11,1... | collective-permute-start | bytes 24584 | tf_op jit(solution)/shard_map/ppermute | solution.py:26
  30.9 5.8 %collective-permute-start.5 = (bf16[1,8,512]{2,1,0:T(8,128)(2,1)S(1)}, bf16[1,8,512]{2,1,0:T(8,128)(2,1)S(1)}, u32[]{:S(2)}, u32[]{:S(2)}) collective-permute-start(bf16[1,8,512]{2,1,0:T(8,128)(2,1)S(1)} %collective-permute-done.4), channel_id=1, source_target_pairs={{0,1},{1,2},{2,3},{3,4},{4,5},{5,6},{6,7},{7,8},{8,9},{9,10},{10,1... | collective-permute-start | bytes 24584 | tf_op jit(solution)/shard_map/ppermute | solution.py:24
  31.8 5.8 %collective-permute-start.12 = (bf16[1,8,512]{2,1,0:T(8,128)(2,1)S(1)}, bf16[1,8,512]{2,1,0:T(8,128)(2,1)S(1)}, u32[]{:S(2)}, u32[]{:S(2)}) collective-permute-start(bf16[1,8,512]{2,1,0:T(8,128)(2,1)S(1)} %collective-permute-done.11), channel_id=1, source_target_pairs={{1,0},{2,1},{3,2},{4,3},{5,4},{6,5},{7,6},{8,7},{9,8},{10,9},{11,1... | collective-permute-start | bytes 24584 | tf_op jit(solution)/shard_map/ppermute | solution.py:26
  36.7 5.8 %collective-permute-start.6 = (bf16[1,8,512]{2,1,0:T(8,128)(2,1)S(1)}, bf16[1,8,512]{2,1,0:T(8,128)(2,1)S(1)}, u32[]{:S(2)}, u32[]{:S(2)}) collective-permute-start(bf16[1,8,512]{2,1,0:T(8,128)(2,1)S(1)} %collective-permute-done.5), channel_id=1, source_target_pairs={{0,1},{1,2},{2,3},{3,4},{4,5},{5,6},{6,7},{7,8},{8,9},{9,10},{10,1... | collective-permute-start | bytes 24584 | tf_op jit(solution)/shard_map/ppermute | solution.py:24
  37.5 31.0 %collective-permute-start.13 = (bf16[1,8,512]{2,1,0:T(8,128)(2,1)S(1)}, bf16[1,8,512]{2,1,0:T(8,128)(2,1)S(1)}, u32[]{:S(2)}, u32[]{:S(2)}) collective-permute-start(bf16[1,8,512]{2,1,0:T(8,128)(2,1)S(1)} %collective-permute-done.12), channel_id=1, source_target_pairs={{1,0},{2,1},{3,2},{4,3},{5,4},{6,5},{7,6},{8,7},{9,8},{10,9},{11,1... | collective-permute-start | bytes 24584 | tf_op jit(solution)/shard_map/ppermute | solution.py:26
  42.4 27.3 %collective-permute-start.7 = (bf16[1,8,512]{2,1,0:T(8,128)(2,1)S(1)}, bf16[1,8,512]{2,1,0:T(8,128)(2,1)S(1)}, u32[]{:S(2)}, u32[]{:S(2)}) collective-permute-start(bf16[1,8,512]{2,1,0:T(8,128)(2,1)S(1)} %collective-permute-done.6), channel_id=1, source_target_pairs={{0,1},{1,2},{2,3},{3,4},{4,5},{5,6},{6,7},{7,8},{8,9},{9,10},{10,1... | collective-permute-start | bytes 24584 | tf_op jit(solution)/shard_map/ppermute | solution.py:24
  68.6 2.5 %collective-permute-start.14 = (bf16[1,8,512]{2,1,0:T(8,128)(2,1)S(1)}, bf16[1,8,512]{2,1,0:T(8,128)(2,1)S(1)}, u32[]{:S(2)}, u32[]{:S(2)}) collective-permute-start(bf16[1,8,512]{2,1,0:T(8,128)(2,1)S(1)} %collective-permute-done.13), channel_id=1, source_target_pairs={{1,0},{2,1},{3,2},{4,3},{5,4},{6,5},{7,6},{8,7},{9,8},{10,9},{11,1... | collective-permute-start | bytes 24584 | tf_op jit(solution)/shard_map/ppermute | solution.py:26
